TPU v7x, 128 devices: a whole 4x4x4 slice. The times are simulated.
128 devices in a mesh: blk: 16 (over x, y_hi, core), grp: 8 (over z, y_lo).
Axes of the slice: x: 4, y: 4 (y_hi: 2, y_lo: 2; y = y_hi * 2 + y_lo), z: 4, core: 2. Of those that a mesh axis runs over, the one named last changes fastest.
Arguments:
- raw_panels: bfloat16 [8, 2048, 8192], P('grp', 'blk'), may hold values from -0.375 to 0.375
- metric: bfloat16 [1024, 1024], replicated, may hold values from -0.1875 to 0.1875
- tile_pairs: int32 [224, 2], P('blk'), may hold values from 0 to 15, as said below
- owners: int32 [224, 1], P('blk'), may hold values from 0 to 15; in each aligned block of 14 rows (0 to 13, 14 to 27, ...) at most 2 rows name the same one
- group_mask: int32 [224, 8], P('blk', 'grp'), may hold values 0 or 1
Outputs:
- owned_tiles: float32 [16, 16, 2, 128, 128], P('blk', None, None, 'grp')
Inputs may be any that keep to these rules, and one draw needn't show every extreme that they name: `tile_pairs`: tile rows of source s (rows s * 14 to s * 14 + 13) have first entry s, the basis block held by index s of blk; the second entry differs from the first. `owners`: in each aligned block of 14 rows (one source) no owner appears more than 2 times.
All inputs are finite; a program needn't handle non-finite values. No bound on the sum of `group_mask` on one device may be relied on, other than what follows from the above.
Results may differ from a plain program's by a relative error of at most 0.0029.
Values may be sent and summed in bfloat16 or wider, within the bound.
A program may use at most 128 MiB of HBM per device.

v0:
```python
import jax
import jax.numpy as jnp
from jax import lax
from jax.sharding import PartitionSpec as P

TILE = 128


def passed_along(value, axis, steps):
    count = lax.axis_size(axis)
    pairs = [(source, (source + steps) % count) for source in range(count)]
    return lax.ppermute(value, axis, pairs)


def per_device(raw_panels, metric, tile_pairs, owners, group_mask):
    raw = raw_panels[0]
    rows = raw.shape[0]
    columns = raw.shape[1]
    naux = metric.shape[0]
    occ = columns // naux
    flat = raw.reshape(rows * occ, naux)
    fitted = lax.dot_general(
        flat, metric, (((1,), (1,)), ((), ())), preferred_element_type=jnp.float32
    )
    panel = fitted.astype(jnp.bfloat16).reshape(rows, columns)
    cycle = lax.axis_size("blk")
    mine = lax.axis_index("blk")
    tile_count = tile_pairs.shape[0]
    capacity = max(2, 2 * tile_count // cycle)
    labels = jnp.arange(cycle)

    def place(total, visiting, source):
        block = lax.dot_general(
            panel, visiting, (((1,), (1,)), ((), ())), preferred_element_type=jnp.float32
        )
        return lax.dynamic_update_slice(total, block, (jnp.int32(0), source * rows))

    start = place(jnp.zeros((rows, cycle * rows), jnp.float32), panel, mine)

    def advance(step, carry):
        visiting, total = carry
        visiting = passed_along(visiting, "blk", 1)
        source = (mine - step) % cycle
        return (visiting, place(total, visiting, source))

    _, row_block = lax.fori_loop(1, cycle, advance, (panel, start))
    local_blocks = rows // TILE
    arranged = jnp.swapaxes(row_block.reshape(local_blocks, TILE, cycle * local_blocks, TILE), 1, 2)
    mu_local = tile_pairs[:, 0] - mine * local_blocks
    picked = arranged[mu_local, tile_pairs[:, 1]]
    weighted = picked * group_mask[:, 0].astype(jnp.float32)[:, None, None]
    owner_ids = owners[:, 0]
    hits = (owner_ids[:, None] == labels[None, :]).astype(jnp.int32)
    before = jnp.cumsum(hits, axis=0) - hits
    slots = jnp.sum(before * hits, axis=1)
    outgoing = (
        jnp.zeros((cycle, capacity, TILE, TILE), jnp.float32).at[owner_ids, slots].set(weighted)
    )
    arrived = lax.all_to_all(outgoing, "blk", split_axis=0, concat_axis=0, tiled=True)
    summed = lax.psum_scatter(arrived, "grp", scatter_dimension=2, tiled=True)
    return summed[None]


def solution(mesh):
    placed = (P("grp", "blk", None), P(), P("blk", None), P("blk", None), P("blk", "grp"))
    return jax.shard_map(
        per_device,
        mesh=mesh,
        in_specs=placed,
        out_specs=P("blk", None, None, "grp", None),
        check_vma=False,
    )
```

profile of v0, /device:TPU:1, one launch (start us, length us, event | category | flops | bytes accessed | tf_op | source)
XLA Modules:
  0.0 653.2 jit_solution(16716808976648020772)
XLA Ops:
  6.5 4.3 reshape_squeeze.3
  10.9 5.3 convolution_convert_fusion
  16.1 4.2 reshape.25
  26.5 499.3 %while.17 = (s32[]{:T(128)}, bf16[128,8192]{1,0:T(8,128)(2,1)}, f32[128,2048]{1,0:T(8,128)S(1)}, bf16[128,8192]{1,0:T(8,128)(2,1)}, s32[]{:T(128)}, /*index=5*/s...) while((s32[]{:T(128)}, bf16[128,8192]{1,0:T(8,128)(2,1)}, ...), condition=%wide.region_3.4_spmd, body=%wide.region_2.3_spmd.sunk | while | flops 268435488 | bytes 25231708 | solution.py:46
  26.5 4.4 collective-permute-start
  30.9 23.3 %collective-permute-done = bf16[128,8192]{1,0:T(8,128)(2,1)} collective-permute-done((bf16[128,8192]{1,0:T(8,128)(2,1)}, bf16[128,8192]{1,0:T(8,128)(2,1)}, u32[]{:S(2)}, u32[]{:S(2)}) %collective-permute-start) | collective-permute-done | bytes 2097184 | tf_op jit(solution)/shard_map/while/body/eval_jaxpr/ppermute | solution.py:12
  59.6 4.1 collective-permute-start
  63.7 23.3 %collective-permute-done = bf16[128,8192]{1,0:T(8,128)(2,1)} collective-permute-done((bf16[128,8192]{1,0:T(8,128)(2,1)}, bf16[128,8192]{1,0:T(8,128)(2,1)}, u32[]{:S(2)}, u32[]{:S(2)}) %collective-permute-start) | collective-permute-done | bytes 2097184 | tf_op jit(solution)/shard_map/while/body/eval_jaxpr/ppermute | solution.py:12
  92.4 4.1 collective-permute-start
  96.4 23.3 %collective-permute-done = bf16[128,8192]{1,0:T(8,128)(2,1)} collective-permute-done((bf16[128,8192]{1,0:T(8,128)(2,1)}, bf16[128,8192]{1,0:T(8,128)(2,1)}, u32[]{:S(2)}, u32[]{:S(2)}) %collective-permute-start) | collective-permute-done | bytes 2097184 | tf_op jit(solution)/shard_map/while/body/eval_jaxpr/ppermute | solution.py:12
  125.2 4.0 collective-permute-start
  129.2 23.3 %collective-permute-done = bf16[128,8192]{1,0:T(8,128)(2,1)} collective-permute-done((bf16[128,8192]{1,0:T(8,128)(2,1)}, bf16[128,8192]{1,0:T(8,128)(2,1)}, u32[]{:S(2)}, u32[]{:S(2)}) %collective-permute-start) | collective-permute-done | bytes 2097184 | tf_op jit(solution)/shard_map/while/body/eval_jaxpr/ppermute | solution.py:12
  157.9 4.1 collective-permute-start
  162.0 23.3 %collective-permute-done = bf16[128,8192]{1,0:T(8,128)(2,1)} collective-permute-done((bf16[128,8192]{1,0:T(8,128)(2,1)}, bf16[128,8192]{1,0:T(8,128)(2,1)}, u32[]{:S(2)}, u32[]{:S(2)}) %collective-permute-start) | collective-permute-done | bytes 2097184 | tf_op jit(solution)/shard_map/while/body/eval_jaxpr/ppermute | solution.py:12
  190.7 4.1 collective-permute-start
  194.8 23.3 %collective-permute-done = bf16[128,8192]{1,0:T(8,128)(2,1)} collective-permute-done((bf16[128,8192]{1,0:T(8,128)(2,1)}, bf16[128,8192]{1,0:T(8,128)(2,1)}, u32[]{:S(2)}, u32[]{:S(2)}) %collective-permute-start) | collective-permute-done | bytes 2097184 | tf_op jit(solution)/shard_map/while/body/eval_jaxpr/ppermute | solution.py:12
  223.5 4.0 collective-permute-start
  227.5 23.3 %collective-permute-done = bf16[128,8192]{1,0:T(8,128)(2,1)} collective-permute-done((bf16[128,8192]{1,0:T(8,128)(2,1)}, bf16[128,8192]{1,0:T(8,128)(2,1)}, u32[]{:S(2)}, u32[]{:S(2)}) %collective-permute-start) | collective-permute-done | bytes 2097184 | tf_op jit(solution)/shard_map/while/body/eval_jaxpr/ppermute | solution.py:12
  256.3 4.1 collective-permute-start
  260.3 23.3 %collective-permute-done = bf16[128,8192]{1,0:T(8,128)(2,1)} collective-permute-done((bf16[128,8192]{1,0:T(8,128)(2,1)}, bf16[128,8192]{1,0:T(8,128)(2,1)}, u32[]{:S(2)}, u32[]{:S(2)}) %collective-permute-start) | collective-permute-done | bytes 2097184 | tf_op jit(solution)/shard_map/while/body/eval_jaxpr/ppermute | solution.py:12
  289.0 4.1 collective-permute-start
  293.1 23.3 %collective-permute-done = bf16[128,8192]{1,0:T(8,128)(2,1)} collective-permute-done((bf16[128,8192]{1,0:T(8,128)(2,1)}, bf16[128,8192]{1,0:T(8,128)(2,1)}, u32[]{:S(2)}, u32[]{:S(2)}) %collective-permute-start) | collective-permute-done | bytes 2097184 | tf_op jit(solution)/shard_map/while/body/eval_jaxpr/ppermute | solution.py:12
  325.9 23.3 %collective-permute-done = bf16[128,8192]{1,0:T(8,128)(2,1)} collective-permute-done((bf16[128,8192]{1,0:T(8,128)(2,1)}, bf16[128,8192]{1,0:T(8,128)(2,1)}, u32[]{:S(2)}, u32[]{:S(2)}) %collective-permute-start) | collective-permute-done | bytes 2097184 | tf_op jit(solution)/shard_map/while/body/eval_jaxpr/ppermute | solution.py:12
  354.6 4.1 collective-permute-start
  358.6 23.3 %collective-permute-done = bf16[128,8192]{1,0:T(8,128)(2,1)} collective-permute-done((bf16[128,8192]{1,0:T(8,128)(2,1)}, bf16[128,8192]{1,0:T(8,128)(2,1)}, u32[]{:S(2)}, u32[]{:S(2)}) %collective-permute-start) | collective-permute-done | bytes 2097184 | tf_op jit(solution)/shard_map/while/body/eval_jaxpr/ppermute | solution.py:12
  387.4 4.1 collective-permute-start
  391.4 24.3 %collective-permute-done = bf16[128,8192]{1,0:T(8,128)(2,1)} collective-permute-done((bf16[128,8192]{1,0:T(8,128)(2,1)}, bf16[128,8192]{1,0:T(8,128)(2,1)}, u32[]{:S(2)}, u32[]{:S(2)}) %collective-permute-start) | collective-permute-done | bytes 2097184 | tf_op jit(solution)/shard_map/while/body/eval_jaxpr/ppermute | solution.py:12
  424.2 26.4 %collective-permute-done = bf16[128,8192]{1,0:T(8,128)(2,1)} collective-permute-done((bf16[128,8192]{1,0:T(8,128)(2,1)}, bf16[128,8192]{1,0:T(8,128)(2,1)}, u32[]{:S(2)}, u32[]{:S(2)}) %collective-permute-start) | collective-permute-done | bytes 2097184 | tf_op jit(solution)/shard_map/while/body/eval_jaxpr/ppermute | solution.py:12
  457.0 28.5 %collective-permute-done = bf16[128,8192]{1,0:T(8,128)(2,1)} collective-permute-done((bf16[128,8192]{1,0:T(8,128)(2,1)}, bf16[128,8192]{1,0:T(8,128)(2,1)}, u32[]{:S(2)}, u32[]{:S(2)}) %collective-permute-start) | collective-permute-done | bytes 2097184 | tf_op jit(solution)/shard_map/while/body/eval_jaxpr/ppermute | solution.py:12
  491.0 29.3 %collective-permute-done = bf16[128,8192]{1,0:T(8,128)(2,1)} collective-permute-done((bf16[128,8192]{1,0:T(8,128)(2,1)}, bf16[128,8192]{1,0:T(8,128)(2,1)}, u32[]{:S(2)}, u32[]{:S(2)}) %collective-permute-start) | collective-permute-done | bytes 2097184 | tf_op jit(solution)/shard_map/while/body/eval_jaxpr/ppermute | solution.py:12
  536.5 57.7 %all_to_all.5 = f32[16,2,128,128]{3,2,1,0:T(8,128)} all-to-all(f32[16,2,128,128]{3,2,1,0:T(8,128)} %scatter_fusion), channel_id=1, replica_groups=mesh['blk'=16,'grp'=8] {'blk'}, dimensions={0} | all-to-all | bytes 4194304 | tf_op jit(solution)/shard_map/all_to_all | solution.py:59
  594.3 52.1 %reduce-scatter.2.cloned.1.call-done = f32[16,2,16,128]{3,2,1,0:T(8,128)} async-done(((f32[16,2,128,128]{3,2,1,0:T(8,128)}), f32[16,2,16,128]{3,2,1,0:T(8,128)}) %reduce-scatter.2.cloned.1.call-update) | async-done | bytes 262160 | tf_op jit(solution)/shard_map/reduce_scatter | solution.py:60
  (89 shorter events, 106.1 us)
Async XLA Ops:
  6.5 4.4 copy-start
  6.5 639.8 %reduce-scatter.2.cloned.1.call-start = ((), (), s32[]{:S(2)}) async-start(), calls=%async_computation.2 | async-start | bytes 2359296 | tf_op jit(solution)/shard_map/reduce_scatter | solution.py:60
  26.5 27.7 %collective-permute-start = (bf16[128,8192]{1,0:T(8,128)(2,1)}, bf16[128,8192]{1,0:T(8,128)(2,1)}, u32[]{:S(2)}, u32[]{:S(2)}) collective-permute-start(bf16[128,8192]{1,0:T(8,128)(2,1)} %get-tuple-element.192), channel_id=1, source_target_pairs={{0,8},{8,16},{16,24},{24,32},{32,40},{40,48},{48,56},{56,64},{64,7... | collective-permute-start | bytes 6291464 | tf_op jit(solution)/shard_map/while/body/eval_jaxpr/ppermute | solution.py:12
  30.9 26.4 %copy-start.1 = (bf16[128,8192]{1,0:T(8,128)(2,1)S(1)}, bf16[128,8192]{1,0:T(8,128)(2,1)}, u32[]{:S(2)}) copy-start(bf16[128,8192]{1,0:T(8,128)(2,1)} %get-tuple-element.205) | copy-start | bytes 6291460 | tf_op jit(solution)/shard_map/while
  59.6 27.4 %collective-permute-start = (bf16[128,8192]{1,0:T(8,128)(2,1)}, bf16[128,8192]{1,0:T(8,128)(2,1)}, u32[]{:S(2)}, u32[]{:S(2)}) collective-permute-start(bf16[128,8192]{1,0:T(8,128)(2,1)} %get-tuple-element.192), channel_id=1, source_target_pairs={{0,8},{8,16},{16,24},{24,32},{32,40},{40,48},{48,56},{56,64},{64,7... | collective-permute-start | bytes 6291464 | tf_op jit(solution)/shard_map/while/body/eval_jaxpr/ppermute | solution.py:12
  63.7 26.4 %copy-start.1 = (bf16[128,8192]{1,0:T(8,128)(2,1)S(1)}, bf16[128,8192]{1,0:T(8,128)(2,1)}, u32[]{:S(2)}) copy-start(bf16[128,8192]{1,0:T(8,128)(2,1)} %get-tuple-element.205) | copy-start | bytes 6291460 | tf_op jit(solution)/shard_map/while
  92.4 27.3 %collective-permute-start = (bf16[128,8192]{1,0:T(8,128)(2,1)}, bf16[128,8192]{1,0:T(8,128)(2,1)}, u32[]{:S(2)}, u32[]{:S(2)}) collective-permute-start(bf16[128,8192]{1,0:T(8,128)(2,1)} %get-tuple-element.192), channel_id=1, source_target_pairs={{0,8},{8,16},{16,24},{24,32},{32,40},{40,48},{48,56},{56,64},{64,7... | collective-permute-start | bytes 6291464 | tf_op jit(solution)/shard_map/while/body/eval_jaxpr/ppermute | solution.py:12
  96.4 26.4 %copy-start.1 = (bf16[128,8192]{1,0:T(8,128)(2,1)S(1)}, bf16[128,8192]{1,0:T(8,128)(2,1)}, u32[]{:S(2)}) copy-start(bf16[128,8192]{1,0:T(8,128)(2,1)} %get-tuple-element.205) | copy-start | bytes 6291460 | tf_op jit(solution)/shard_map/while
  125.2 27.3 %collective-permute-start = (bf16[128,8192]{1,0:T(8,128)(2,1)}, bf16[128,8192]{1,0:T(8,128)(2,1)}, u32[]{:S(2)}, u32[]{:S(2)}) collective-permute-start(bf16[128,8192]{1,0:T(8,128)(2,1)} %get-tuple-element.192), channel_id=1, source_target_pairs={{0,8},{8,16},{16,24},{24,32},{32,40},{40,48},{48,56},{56,64},{64,7... | collective-permute-start | bytes 6291464 | tf_op jit(solution)/shard_map/while/body/eval_jaxpr/ppermute | solution.py:12
  129.2 26.4 %copy-start.1 = (bf16[128,8192]{1,0:T(8,128)(2,1)S(1)}, bf16[128,8192]{1,0:T(8,128)(2,1)}, u32[]{:S(2)}) copy-start(bf16[128,8192]{1,0:T(8,128)(2,1)} %get-tuple-element.205) | copy-start | bytes 6291460 | tf_op jit(solution)/shard_map/while
  157.9 27.3 %collective-permute-start = (bf16[128,8192]{1,0:T(8,128)(2,1)}, bf16[128,8192]{1,0:T(8,128)(2,1)}, u32[]{:S(2)}, u32[]{:S(2)}) collective-permute-start(bf16[128,8192]{1,0:T(8,128)(2,1)} %get-tuple-element.192), channel_id=1, source_target_pairs={{0,8},{8,16},{16,24},{24,32},{32,40},{40,48},{48,56},{56,64},{64,7... | collective-permute-start | bytes 6291464 | tf_op jit(solution)/shard_map/while/body/eval_jaxpr/ppermute | solution.py:12
  162.0 26.4 %copy-start.1 = (bf16[128,8192]{1,0:T(8,128)(2,1)S(1)}, bf16[128,8192]{1,0:T(8,128)(2,1)}, u32[]{:S(2)}) copy-start(bf16[128,8192]{1,0:T(8,128)(2,1)} %get-tuple-element.205) | copy-start | bytes 6291460 | tf_op jit(solution)/shard_map/while
  190.7 27.3 %collective-permute-start = (bf16[128,8192]{1,0:T(8,128)(2,1)}, bf16[128,8192]{1,0:T(8,128)(2,1)}, u32[]{:S(2)}, u32[]{:S(2)}) collective-permute-start(bf16[128,8192]{1,0:T(8,128)(2,1)} %get-tuple-element.192), channel_id=1, source_target_pairs={{0,8},{8,16},{16,24},{24,32},{32,40},{40,48},{48,56},{56,64},{64,7... | collective-permute-start | bytes 6291464 | tf_op jit(solution)/shard_map/while/body/eval_jaxpr/ppermute | solution.py:12
  194.8 26.4 %copy-start.1 = (bf16[128,8192]{1,0:T(8,128)(2,1)S(1)}, bf16[128,8192]{1,0:T(8,128)(2,1)}, u32[]{:S(2)}) copy-start(bf16[128,8192]{1,0:T(8,128)(2,1)} %get-tuple-element.205) | copy-start | bytes 6291460 | tf_op jit(solution)/shard_map/while
  223.5 27.3 %collective-permute-start = (bf16[128,8192]{1,0:T(8,128)(2,1)}, bf16[128,8192]{1,0:T(8,128)(2,1)}, u32[]{:S(2)}, u32[]{:S(2)}) collective-permute-start(bf16[128,8192]{1,0:T(8,128)(2,1)} %get-tuple-element.192), channel_id=1, source_target_pairs={{0,8},{8,16},{16,24},{24,32},{32,40},{40,48},{48,56},{56,64},{64,7... | collective-permute-start | bytes 6291464 | tf_op jit(solution)/shard_map/while/body/eval_jaxpr/ppermute | solution.py:12
  227.5 26.4 %copy-start.1 = (bf16[128,8192]{1,0:T(8,128)(2,1)S(1)}, bf16[128,8192]{1,0:T(8,128)(2,1)}, u32[]{:S(2)}) copy-start(bf16[128,8192]{1,0:T(8,128)(2,1)} %get-tuple-element.205) | copy-start | bytes 6291460 | tf_op jit(solution)/shard_map/while
  256.3 27.3 %collective-permute-start = (bf16[128,8192]{1,0:T(8,128)(2,1)}, bf16[128,8192]{1,0:T(8,128)(2,1)}, u32[]{:S(2)}, u32[]{:S(2)}) collective-permute-start(bf16[128,8192]{1,0:T(8,128)(2,1)} %get-tuple-element.192), channel_id=1, source_target_pairs={{0,8},{8,16},{16,24},{24,32},{32,40},{40,48},{48,56},{56,64},{64,7... | collective-permute-start | bytes 6291464 | tf_op jit(solution)/shard_map/while/body/eval_jaxpr/ppermute | solution.py:12
  260.3 26.4 %copy-start.1 = (bf16[128,8192]{1,0:T(8,128)(2,1)S(1)}, bf16[128,8192]{1,0:T(8,128)(2,1)}, u32[]{:S(2)}) copy-start(bf16[128,8192]{1,0:T(8,128)(2,1)} %get-tuple-element.205) | copy-start | bytes 6291460 | tf_op jit(solution)/shard_map/while
  289.0 27.3 %collective-permute-start = (bf16[128,8192]{1,0:T(8,128)(2,1)}, bf16[128,8192]{1,0:T(8,128)(2,1)}, u32[]{:S(2)}, u32[]{:S(2)}) collective-permute-start(bf16[128,8192]{1,0:T(8,128)(2,1)} %get-tuple-element.192), channel_id=1, source_target_pairs={{0,8},{8,16},{16,24},{24,32},{32,40},{40,48},{48,56},{56,64},{64,7... | collective-permute-start | bytes 6291464 | tf_op jit(solution)/shard_map/while/body/eval_jaxpr/ppermute | solution.py:12
  293.1 26.4 %copy-start.1 = (bf16[128,8192]{1,0:T(8,128)(2,1)S(1)}, bf16[128,8192]{1,0:T(8,128)(2,1)}, u32[]{:S(2)}) copy-start(bf16[128,8192]{1,0:T(8,128)(2,1)} %get-tuple-element.205) | copy-start | bytes 6291460 | tf_op jit(solution)/shard_map/while
  321.8 27.3 %collective-permute-start = (bf16[128,8192]{1,0:T(8,128)(2,1)}, bf16[128,8192]{1,0:T(8,128)(2,1)}, u32[]{:S(2)}, u32[]{:S(2)}) collective-permute-start(bf16[128,8192]{1,0:T(8,128)(2,1)} %get-tuple-element.192), channel_id=1, source_target_pairs={{0,8},{8,16},{16,24},{24,32},{32,40},{40,48},{48,56},{56,64},{64,7... | collective-permute-start | bytes 6291464 | tf_op jit(solution)/shard_map/while/body/eval_jaxpr/ppermute | solution.py:12
  325.9 26.4 %copy-start.1 = (bf16[128,8192]{1,0:T(8,128)(2,1)S(1)}, bf16[128,8192]{1,0:T(8,128)(2,1)}, u32[]{:S(2)}) copy-start(bf16[128,8192]{1,0:T(8,128)(2,1)} %get-tuple-element.205) | copy-start | bytes 6291460 | tf_op jit(solution)/shard_map/while
  354.6 27.3 %collective-permute-start = (bf16[128,8192]{1,0:T(8,128)(2,1)}, bf16[128,8192]{1,0:T(8,128)(2,1)}, u32[]{:S(2)}, u32[]{:S(2)}) collective-permute-start(bf16[128,8192]{1,0:T(8,128)(2,1)} %get-tuple-element.192), channel_id=1, source_target_pairs={{0,8},{8,16},{16,24},{24,32},{32,40},{40,48},{48,56},{56,64},{64,7... | collective-permute-start | bytes 6291464 | tf_op jit(solution)/shard_map/while/body/eval_jaxpr/ppermute | solution.py:12
  358.6 26.4 %copy-start.1 = (bf16[128,8192]{1,0:T(8,128)(2,1)S(1)}, bf16[128,8192]{1,0:T(8,128)(2,1)}, u32[]{:S(2)}) copy-start(bf16[128,8192]{1,0:T(8,128)(2,1)} %get-tuple-element.205) | copy-start | bytes 6291460 | tf_op jit(solution)/shard_map/while
  387.4 28.4 %collective-permute-start = (bf16[128,8192]{1,0:T(8,128)(2,1)}, bf16[128,8192]{1,0:T(8,128)(2,1)}, u32[]{:S(2)}, u32[]{:S(2)}) collective-permute-start(bf16[128,8192]{1,0:T(8,128)(2,1)} %get-tuple-element.192), channel_id=1, source_target_pairs={{0,8},{8,16},{16,24},{24,32},{32,40},{40,48},{48,56},{56,64},{64,7... | collective-permute-start | bytes 6291464 | tf_op jit(solution)/shard_map/while/body/eval_jaxpr/ppermute | solution.py:12
  391.4 27.4 %copy-start.1 = (bf16[128,8192]{1,0:T(8,128)(2,1)S(1)}, bf16[128,8192]{1,0:T(8,128)(2,1)}, u32[]{:S(2)}) copy-start(bf16[128,8192]{1,0:T(8,128)(2,1)} %get-tuple-element.205) | copy-start | bytes 6291460 | tf_op jit(solution)/shard_map/while
  421.1 29.5 %collective-permute-start = (bf16[128,8192]{1,0:T(8,128)(2,1)}, bf16[128,8192]{1,0:T(8,128)(2,1)}, u32[]{:S(2)}, u32[]{:S(2)}) collective-permute-start(bf16[128,8192]{1,0:T(8,128)(2,1)} %get-tuple-element.192), channel_id=1, source_target_pairs={{0,8},{8,16},{16,24},{24,32},{32,40},{40,48},{48,56},{56,64},{64,7... | collective-permute-start | bytes 6291464 | tf_op jit(solution)/shard_map/while/body/eval_jaxpr/ppermute | solution.py:12
  424.2 29.5 %copy-start.1 = (bf16[128,8192]{1,0:T(8,128)(2,1)S(1)}, bf16[128,8192]{1,0:T(8,128)(2,1)}, u32[]{:S(2)}) copy-start(bf16[128,8192]{1,0:T(8,128)(2,1)} %get-tuple-element.205) | copy-start | bytes 6291460 | tf_op jit(solution)/shard_map/while
  456.0 29.5 %collective-permute-start = (bf16[128,8192]{1,0:T(8,128)(2,1)}, bf16[128,8192]{1,0:T(8,128)(2,1)}, u32[]{:S(2)}, u32[]{:S(2)}) collective-permute-start(bf16[128,8192]{1,0:T(8,128)(2,1)} %get-tuple-element.192), channel_id=1, source_target_pairs={{0,8},{8,16},{16,24},{24,32},{32,40},{40,48},{48,56},{56,64},{64,7... | collective-permute-start | bytes 6291464 | tf_op jit(solution)/shard_map/while/body/eval_jaxpr/ppermute | solution.py:12
  457.0 31.6 %copy-start.1 = (bf16[128,8192]{1,0:T(8,128)(2,1)S(1)}, bf16[128,8192]{1,0:T(8,128)(2,1)}, u32[]{:S(2)}) copy-start(bf16[128,8192]{1,0:T(8,128)(2,1)} %get-tuple-element.205) | copy-start | bytes 6291460 | tf_op jit(solution)/shard_map/while
  490.9 29.5 %collective-permute-start = (bf16[128,8192]{1,0:T(8,128)(2,1)}, bf16[128,8192]{1,0:T(8,128)(2,1)}, u32[]{:S(2)}, u32[]{:S(2)}) collective-permute-start(bf16[128,8192]{1,0:T(8,128)(2,1)} %get-tuple-element.192), channel_id=1, source_target_pairs={{0,8},{8,16},{16,24},{24,32},{32,40},{40,48},{48,56},{56,64},{64,7... | collective-permute-start | bytes 6291464 | tf_op jit(solution)/shard_map/while/body/eval_jaxpr/ppermute | solution.py:12
  491.0 32.5 %copy-start.1 = (bf16[128,8192]{1,0:T(8,128)(2,1)S(1)}, bf16[128,8192]{1,0:T(8,128)(2,1)}, u32[]{:S(2)}) copy-start(bf16[128,8192]{1,0:T(8,128)(2,1)} %get-tuple-element.205) | copy-start | bytes 6291460 | tf_op jit(solution)/shard_map/while
  (3 other events, 8.8 us)
Sparse Core Ops, SparseCore 0:
  594.4 51.9 reduce-scatter.1
where the time goes:
time: 655 us; the launch traced here: 653 us
  waiting for transfers between devices  417 us (64%)
  local copies, waits for them, and re-layouts  67.5 us (10%)
  blocking collectives  57.7 us (9%)
  starting transfers between devices  53 us (8%)
  matrix products  42.7 us (7%)
  between operations  13.5 us (2%)
    ppermute x15, waiting for transfers between devices, passed_along(): return lax.ppermute(value, axis, pairs)  365 us
    all_to_all x1, blocking collectives, per_device(): lax.all_to_all(outgoing, 'blk', split_axis=0, concat_axis=0, tiled=True)  57.7 us
    ppermute x15, starting transfers between devices, passed_along(): return lax.ppermute(value, axis, pairs)  53 us
    reduce_scatter x1, waiting for transfers between devices, per_device(): summed = lax.psum_scatter(arrived, 'grp', scatter_dimension=2, tiled=True)  52.1 us
    while x45, local copies, waits for them, and re-layouts  46.6 us
    dot_general x16, matrix products, place(): lax.dot_general(panel, visiting, (((1,), (1,)), ((), ())), preferred_elem...  37.4 us
  transfers between devices with their start and end apart: 16, of which 16 were waited for; matrix products, arithmetic and copies ran while one was open for 0% of the time, Pallas kernels for 0%

commit v1 on v0

v1 whole, which is shorter than its diff:
```python
import jax
import jax.numpy as jnp
from jax import lax
from jax.experimental import pallas as pl
from jax.experimental.pallas import tpu as pltpu
from jax.sharding import PartitionSpec as P

MESH = pl.DeviceIdType.MESH
F32, BF16 = jnp.float32, jnp.bfloat16

CHIPS = 8
BLKS = 16
GRPS = 8
T = 128
K = 1024
HALF = 8
SLOTS = 2
ROWS = T // GRPS


def dot_t(a, b):
    return lax.dot_general(a, b, (((1,), (1,)), ((), ())), preferred_element_type=F32)


def kernel(
    raw, metric, pairs, owners, mask, out,
    met, rbuf, fbuf, sbuf, pbuf, xs, xall, ybuf, zbuf, acc, obuf, tbl,
    msem, lsem, asend, arecv, fsend, frecv, psend, precv, xsend, xrecv, ysend, yrecv, osend, orecv, osem,
):
    me = lax.axis_index("blk")
    grp = lax.axis_index("grp")
    chip, core = me // 2, me % 2
    cx, cy = chip // 2, chip % 2
    tiles = pairs.shape[1]

    def chip_to(k):
        return ((cx + k // 2) % 4) * 2 + (cy + k % 2) % 2

    def chip_from(k):
        return ((cx + 4 - k // 2) % 4) * 2 + (cy + k % 2) % 2

    fetch_metric = pltpu.make_async_copy(metric, met, msem)
    fetch_metric.start()
    own = pltpu.make_async_copy(raw.at[:, pl.ds(pl.multiple_of(chip * K, K), K)], rbuf.at[0], lsem)
    own.start()

    barrier = pltpu.get_barrier_semaphore()
    for step in range(1, BLKS):
        pl.semaphore_signal(barrier, inc=1, device_id=((me + step) % BLKS, grp), device_id_type=MESH)
    for step in range(1, GRPS):
        pl.semaphore_signal(barrier, inc=1, device_id=(me, (grp + step) % GRPS), device_id_type=MESH)
    pl.semaphore_wait(barrier, BLKS - 1 + GRPS - 1)

    def raw_copy(k):
        target = chip_to(k)
        return pltpu.make_async_remote_copy(
            src_ref=raw.at[:, pl.ds(pl.multiple_of(target * K, K), K)],
            dst_ref=rbuf.at[k],
            send_sem=asend.at[k],
            recv_sem=arecv.at[k],
            device_id=(target * 2 + core, grp),
            device_id_type=MESH,
        )

    for k in range(1, CHIPS):
        raw_copy(k).start()

    def find(o, carry):
        seen, first, second = jnp.int32(0), jnp.int32(tiles), jnp.int32(tiles)
        for t in range(tiles):
            hit = (owners[0, t] == o).astype(jnp.int32)
            first = first + hit * (seen == 0).astype(jnp.int32) * (t - tiles)
            second = second + hit * (seen == 1).astype(jnp.int32) * (t - tiles)
            seen = seen + hit
        tbl[o * 2] = first
        tbl[o * 2 + 1] = second
        return carry

    lax.fori_loop(0, BLKS, find, 0)

    def fitted_copy(k):
        block = fbuf.at[chip_from(k) * 2 + core]
        return pltpu.make_async_remote_copy(
            src_ref=block,
            dst_ref=block,
            send_sem=fsend.at[k],
            recv_sem=frecv.at[k],
            device_id=(chip * 2 + 1 - core, grp),
            device_id_type=MESH,
        )

    def fitted_arrival(k):
        block = fbuf.at[chip_from(k) * 2 + 1 - core]
        return pltpu.make_async_remote_copy(
            src_ref=block,
            dst_ref=block,
            send_sem=fsend.at[k],
            recv_sem=frecv.at[k],
            device_id=(chip * 2 + 1 - core, grp),
            device_id_type=MESH,
        )

    fetch_metric.wait()
    own.wait()

    def fit(k, carry):
        @pl.when(k > 0)
        def _():
            raw_copy(k).wait_recv()

        fbuf[chip_from(k) * 2 + core] = dot_t(rbuf[k], met[...]).astype(BF16)
        fitted_copy(k).start()
        return carry

    lax.fori_loop(0, CHIPS, fit, 0)
    for k in range(CHIPS):
        fitted_arrival(k).wait_recv()

    def partial_copy(k):
        return pltpu.make_async_remote_copy(
            src_ref=sbuf.at[k],
            dst_ref=pbuf.at[k],
            send_sem=psend.at[k],
            recv_sem=precv.at[k],
            device_id=(chip_to(k) * 2 + core, grp),
            device_id_type=MESH,
        )

    def multiply(step, carry):
        k = CHIPS - 1 - step
        reducer = chip_to(k) * 2 + core
        right = fbuf[reducer]
        for j in range(1, HALF + 1):
            sbuf[k, j - 1] = dot_t(fbuf[(reducer + j) % BLKS], right).astype(BF16)

        @pl.when(k > 0)
        def _():
            partial_copy(k).start()

        return carry

    lax.fori_loop(0, CHIPS, multiply, 0)

    def cross_copy(j):
        return pltpu.make_async_remote_copy(
            src_ref=xs.at[j],
            dst_ref=xall.at[j],
            send_sem=xsend.at[j],
            recv_sem=xrecv.at[j],
            device_id=((me + j) % BLKS, grp),
            device_id_type=MESH,
        )

    for k in range(1, CHIPS):
        partial_copy(k).wait_recv()
    for j in range(1, HALF + 1):
        total = sbuf[0, j - 1].astype(F32)
        for k in range(1, CHIPS):
            total = total + pbuf[k, j - 1].astype(F32)
        if j < HALF:
            xs[j] = total.astype(BF16)
            cross_copy(j).start()
        xall[BLKS - j] = total.T.astype(BF16)
    for j in range(1, HALF):
        cross_copy(j).wait_recv()

    def slice_copy(step):
        target = (grp + step) % GRPS
        return pltpu.make_async_remote_copy(
            src_ref=ybuf.at[target],
            dst_ref=zbuf.at[step],
            send_sem=ysend.at[step],
            recv_sem=yrecv.at[step],
            device_id=(me, target),
            device_id_type=MESH,
        )

    for t in range(tiles):
        picked = xall[(me - pairs[1, t] + BLKS) % BLKS].astype(F32) * mask[0, t].astype(F32)
        ybuf[:, t] = picked.astype(BF16).reshape(GRPS, ROWS, T)
    for step in range(1, GRPS):
        slice_copy(step).start()
    for step in range(1, GRPS):
        slice_copy(step).wait_recv()
    total = ybuf[grp].astype(F32)
    for step in range(1, GRPS):
        total = total + zbuf[step].astype(F32)
    acc[0:tiles] = total
    acc[tiles] = jnp.zeros((ROWS, T), F32)

    def owned_copy(step):
        target = (me + step) % BLKS
        return pltpu.make_async_remote_copy(
            src_ref=obuf.at[target],
            dst_ref=out.at[0, me],
            send_sem=osend.at[step],
            recv_sem=orecv.at[step],
            device_id=(target, grp),
            device_id_type=MESH,
        )

    def owned_arrival(step):
        source = (me + BLKS - step) % BLKS
        return pltpu.make_async_remote_copy(
            src_ref=obuf.at[source],
            dst_ref=out.at[0, source],
            send_sem=osend.at[step],
            recv_sem=orecv.at[step],
            device_id=(source, grp),
            device_id_type=MESH,
        )

    for o in range(BLKS):
        for c in range(SLOTS):
            obuf[o, c] = acc[tbl[o * 2 + c]]
    for step in range(1, BLKS):
        owned_copy(step).start()
    keep = pltpu.make_async_copy(obuf.at[me], out.at[0, me], osem)
    keep.start()

    for k in range(1, CHIPS):
        raw_copy(k).wait_send()
        partial_copy(k).wait_send()
    for k in range(CHIPS):
        fitted_copy(k).wait_send()
    for j in range(1, HALF):
        cross_copy(j).wait_send()
    for step in range(1, GRPS):
        slice_copy(step).wait_send()
    keep.wait()
    for step in range(1, BLKS):
        owned_arrival(step).wait_recv()
        owned_copy(step).wait_send()


def per_device(raw_panels, metric, tile_pairs, owners, group_mask):
    tiles = tile_pairs.shape[0]
    dma = pltpu.SemaphoreType.DMA
    any_space = pl.BlockSpec(memory_space=pl.ANY)
    smem = pl.BlockSpec(memory_space=pltpu.SMEM)
    return pl.pallas_call(
        kernel,
        out_shape=jax.ShapeDtypeStruct((1, BLKS, SLOTS, ROWS, T), F32),
        in_specs=[any_space, any_space, smem, smem, smem],
        out_specs=any_space,
        scratch_shapes=[
            pltpu.VMEM((K, K), BF16),
            pltpu.VMEM((CHIPS, T, K), BF16),
            pltpu.VMEM((BLKS, T, K), BF16),
            pltpu.VMEM((CHIPS, HALF, T, T), BF16),
            pltpu.VMEM((CHIPS, HALF, T, T), BF16),
            pltpu.VMEM((HALF, T, T), BF16),
            pltpu.VMEM((BLKS, T, T), BF16),
            pltpu.VMEM((GRPS, tiles, ROWS, T), BF16),
            pltpu.VMEM((GRPS, tiles, ROWS, T), BF16),
            pltpu.VMEM((tiles + 1, ROWS, T), F32),
            pltpu.VMEM((BLKS, SLOTS, ROWS, T), F32),
            pltpu.SMEM((BLKS * SLOTS,), jnp.int32),
            dma(()), dma(()),
            dma((CHIPS,)), dma((CHIPS,)),
            dma((CHIPS,)), dma((CHIPS,)),
            dma((CHIPS,)), dma((CHIPS,)),
            dma((HALF,)), dma((HALF,)),
            dma((GRPS,)), dma((GRPS,)),
            dma((BLKS,)), dma((BLKS,)),
            dma(()),
        ],
        compiler_params=pltpu.CompilerParams(collective_id=0, has_side_effects=True, vmem_limit_bytes=60 << 20),
        name="exchange",
    )(raw_panels[0], metric, tile_pairs.T, owners.T, group_mask.T)


def solution(mesh):
    placed = (P("grp", "blk", None), P(), P("blk", None), P("blk", None), P("blk", "grp"))
    return jax.shard_map(
        per_device,
        mesh=mesh,
        in_specs=placed,
        out_specs=P("blk", None, None, "grp", None),
        check_vma=False,
    )
```

time: 655 us -> 99.3 us (0.15)
  waiting for transfers between devices: 417 us -> 0 us
  Pallas kernels: 0 us -> 97.5 us
  local copies, waits for them, and re-layouts: 67.5 us -> 1.67 us
  blocking collectives: 57.7 us -> 0 us
  starting transfers between devices: 53 us -> 0 us
  matrix products: 42.7 us -> 0 us
  between operations: 13.5 us -> 0.01 us
    ppermute x15 -> x0, waiting for transfers between devices: 365 us -> none  [passed_along(): return lax.ppermute(value, axis, pairs)]
    pallas_call x0 -> x1, Pallas kernels: none -> 97.5 us  [per_device(): pl.pallas_call(kernel, out_shape=jax.ShapeDtypeStruct((1, BLKS, SLOTS, RO...]
    all_to_all x1 -> x0, blocking collectives: 57.7 us -> none  [per_device(): lax.all_to_all(outgoing, 'blk', split_axis=0, concat_axis=0, tiled=True)]
    ppermute x15 -> x0, starting transfers between devices: 53 us -> none  [passed_along(): return lax.ppermute(value, axis, pairs)]
    reduce_scatter x1 -> x0, waiting for transfers between devices: 52.1 us -> none  [per_device(): summed = lax.psum_scatter(arrived, 'grp', scatter_dimension=2, tiled=True)]
    while x46 -> x0, local copies, waits for them, and re-layouts: 48 us -> none
    dot_general x17 -> x0, matrix products: 42.7 us -> none  [the longest x16 37.4 us: place(): lax.dot_general(panel, visiting, (((1,), (1,)), ((), ())), preferred_elem...]
  transfers between devices with their start and end apart: 16 -> 0, of which waited for: 16 -> 0; matrix products, arithmetic and copies ran while one was open for 0% -> 0% of each run, Pallas kernels for 0% -> 0%
where the time goes in v1:
time: 99.3 us; the launch traced here: 99.2 us
  Pallas kernels  97.5 us (98%)
  local copies, waits for them, and re-layouts  1.67 us (2%)
    pallas_call x1, Pallas kernels, per_device(): pl.pallas_call(kernel, out_shape=jax.ShapeDtypeStruct((1, BLKS, SLOTS, RO...  97.5 us

profile of v1, /device:TPU:1, one launch (start us, length us, event | category | flops | bytes accessed | tf_op | source)
XLA Modules:
  0.0 99.2 jit_solution(3775860730291134885)
XLA Ops:
  0.0 97.5 %exchange.1 = f32[1,16,2,16,128]{4,3,2,1,0:T(8,128)} custom-call(bf16[128,8192]{1,0:T(8,128)(2,1)} %bitcast.4, bf16[1024,1024]{1,0:T(8,128)(2,1)} %metric.1, s32[2,14]{1,0:T(2,128)} %bitcast.5, s32[1,14]{1,0:T(1,128)} %bitcast.6, s32[1,14]{1,0:T(1,128)} %bitcast.7), custom_call_target="tpu_custom_call" | custom-call | tf_op jit(solution)/shard_map/exchange/pallas_call | solution.py:241
  97.5 1.7 %copy.7 = f32[1,16,2,16,128]{4,3,2,1,0:T(8,128)} copy(f32[1,16,2,16,128]{4,3,2,1,0:T(8,128)} %exchange.1) | data formatting | bytes 524288

commit v2 on v1

v2 whole, which is shorter than its diff:
```python
import jax
import jax.numpy as jnp
from jax import lax
from jax.experimental import pallas as pl
from jax.experimental.pallas import tpu as pltpu
from jax.sharding import PartitionSpec as P

MESH = pl.DeviceIdType.MESH
F32, BF16 = jnp.float32, jnp.bfloat16

CHIPS = 8
BLKS = 16
GRPS = 8
T = 128
K = 1024
HALF = 8
SLOTS = 2
ROWS = T // GRPS
PARTS = 4
PART = T // PARTS
NEAR = (2, 6, 1, 5, 3, 7, 4)
ORDER = (2, 4, 6, 1, 3, 5, 7, 8)
STARTS = (0, 2, 4, 7, 8)
QS = len(STARTS) - 1
LIMIT = 60


def dot_t(a, b):
    return lax.dot_general(a, b, (((1,), (1,)), ((), ())), preferred_element_type=F32)


def kernel(
    raw, metric, pairs, owners, mask, out,
    met, rbuf, fbuf, sbuf, pbuf, xs, xall, zbuf, acc, obuf, mvec, msc, tbl, place,
    msem, lsem, vsem, asend, arecv, fsend, frecv, psend, precv, xsend, xrecv, ysend, yrecv, osend, orecv, ksend, krecv, osem,
):
    me = lax.axis_index("blk")
    grp = lax.axis_index("grp")
    chip, core = me // 2, me % 2
    cx, cy = chip // 2, chip % 2
    tiles = pairs.shape[1]

    def chip_to(k):
        return ((cx + k // 2) % 4) * 2 + (cy + k % 2) % 2

    def chip_from(k):
        return ((cx + 4 - k // 2) % 4) * 2 + (cy + k % 2) % 2

    fetch_metric = pltpu.make_async_copy(metric, met, msem)
    fetch_metric.start()
    own = pltpu.make_async_copy(raw.at[:, pl.ds(pl.multiple_of(chip * K, K), K)], rbuf.at[0], lsem)
    own.start()
    own_mask = pltpu.make_async_copy(mask, mvec.at[0], vsem)
    own_mask.start()

    barrier = pltpu.get_barrier_semaphore()
    for step in range(1, BLKS):
        pl.semaphore_signal(barrier, inc=1, device_id=((me + step) % BLKS, grp), device_id_type=MESH)
    for step in range(1, GRPS):
        pl.semaphore_signal(barrier, inc=1, device_id=(me, (grp + step) % GRPS), device_id_type=MESH)
    pl.semaphore_wait(barrier, BLKS - 1 + GRPS - 1)

    def raw_copy(part, k):
        target = chip_to(k)
        rows = pl.ds(pl.multiple_of(part * PART, PART), PART)
        return pltpu.make_async_remote_copy(
            src_ref=raw.at[rows, pl.ds(pl.multiple_of(target * K, K), K)],
            dst_ref=rbuf.at[k, rows],
            send_sem=asend.at[part, k],
            recv_sem=arecv.at[part, k],
            device_id=(target * 2 + core, grp),
            device_id_type=MESH,
        )

    for part in range(PARTS):
        for k in NEAR:
            raw_copy(part, k).start()

    def mask_copy(step):
        return pltpu.make_async_remote_copy(
            src_ref=mask,
            dst_ref=mvec.at[step],
            send_sem=ksend.at[step],
            recv_sem=krecv.at[step],
            device_id=(me, (grp + step) % GRPS),
            device_id_type=MESH,
        )

    for step in range(1, GRPS):
        mask_copy(step).start()

    def find(o, carry):
        seen, first, second = jnp.int32(0), jnp.int32(tiles), jnp.int32(tiles)
        for t in range(tiles):
            hit = (owners[0, t] == o).astype(jnp.int32)
            first = first + hit * (seen == 0).astype(jnp.int32) * (t - tiles)
            second = second + hit * (seen == 1).astype(jnp.int32) * (t - tiles)
            seen = seen + hit
        tbl[o * 2] = first
        tbl[o * 2 + 1] = second
        return carry

    lax.fori_loop(0, BLKS, find, 0)
    place[0] = 0
    for u, j in enumerate(ORDER):
        place[j] = u
        if j < HALF:
            place[BLKS - j] = HALF + u

    def fitted_copy(part, parity):
        rows = fbuf.at[:, parity, pl.ds(pl.multiple_of(part * PART, PART), PART)]
        return pltpu.make_async_remote_copy(
            src_ref=rows,
            dst_ref=rows,
            send_sem=fsend.at[part],
            recv_sem=frecv.at[part],
            device_id=(chip * 2 + 1 - core, grp),
            device_id_type=MESH,
        )

    fetch_metric.wait()
    own.wait()

    def fit(part, carry):
        for k in NEAR:
            raw_copy(part, k).wait_recv()
        rows = pl.ds(pl.multiple_of(part * PART, PART), PART)
        fitted = dot_t(rbuf[:, rows, :].reshape(CHIPS * PART, K), met[...]).astype(BF16).reshape(CHIPS, PART, K)
        for k in range(CHIPS):
            fbuf[chip_from(k), core, rows, :] = fitted[k]
        fitted_copy(part, core).start()
        return carry

    lax.fori_loop(0, PARTS, fit, 0)

    def partial_copy(q, k):
        which = pl.ds(STARTS[q], STARTS[q + 1] - STARTS[q])
        return pltpu.make_async_remote_copy(
            src_ref=sbuf.at[k, which],
            dst_ref=pbuf.at[k, which],
            send_sem=psend.at[q, k],
            recv_sem=precv.at[q, k],
            device_id=(chip_to(k) * 2 + core, grp),
            device_id_type=MESH,
        )

    def products(q):
        def multiply(step, carry):
            k = (step + 1) % CHIPS
            target = chip_to(k)
            reducer = target * 2 + core
            right = fbuf[target, core]
            for u in range(STARTS[q], STARTS[q + 1]):
                block = (reducer + ORDER[u]) % BLKS
                sbuf[k, u] = dot_t(fbuf[block // 2, block % 2], right).astype(BF16)

            @pl.when(k > 0)
            def _():
                partial_copy(q, k).start()

            return carry

        lax.fori_loop(0, CHIPS, multiply, 0)

    def cross_copy(u):
        return pltpu.make_async_remote_copy(
            src_ref=xs.at[u],
            dst_ref=xall.at[HALF + u],
            send_sem=xsend.at[u],
            recv_sem=xrecv.at[u],
            device_id=((me + ORDER[u]) % BLKS, grp),
            device_id_type=MESH,
        )

    def slice_copy(n, first, last, step):
        target = (grp + step) % GRPS
        which = pl.ds(first, last - first)
        return pltpu.make_async_remote_copy(
            src_ref=xall.at[which, pl.ds(pl.multiple_of(target * ROWS, ROWS), ROWS)],
            dst_ref=zbuf.at[step, which],
            send_sem=ysend.at[n, step],
            recv_sem=yrecv.at[n, step],
            device_id=(me, target),
            device_id_type=MESH,
        )

    slices = []

    def send_slices(first, last):
        n = len(slices)
        slices.append((n, first, last))
        for step in range(1, GRPS):
            slice_copy(n, first, last, step).start()

    def reduce(q):
        for k in NEAR:
            partial_copy(q, k).wait_recv()
        for u in range(STARTS[q], STARTS[q + 1]):
            total = sbuf[0, u].astype(F32)
            for k in range(1, CHIPS):
                total = total + pbuf[k, u].astype(F32)
            if ORDER[u] < HALF:
                xs[u] = total.astype(BF16)
                cross_copy(u).start()
            xall[u] = total.T.astype(BF16)
        send_slices(STARTS[q], STARTS[q + 1])

    def crossed(q):
        for u in range(STARTS[q], STARTS[q + 1]):
            cross_copy(u).wait_recv()
        send_slices(HALF + STARTS[q], HALF + STARTS[q + 1])

    products(0)
    for part in range(PARTS):
        fitted_copy(part, 1 - core).wait_recv()
    for q in range(1, QS):
        products(q)
    for q in range(QS):
        reduce(q)
        if q > 0:
            crossed(q - 1)

    for step in range(1, GRPS):
        mask_copy(step).wait_recv()
    own_mask.wait()
    masks = pltpu.make_async_copy(mvec, msc, vsem)
    masks.start()
    masks.wait()
    for n, first, last in slices:
        for step in range(1, GRPS):
            slice_copy(n, first, last, step).wait_recv()
    own_rows = pl.ds(pl.multiple_of(grp * ROWS, ROWS), ROWS)
    for t in range(tiles):
        at = place[(pairs[1, t] - me + BLKS) % BLKS]
        total = xall[at, own_rows, :].astype(F32) * msc[0, 0, t].astype(F32)
        for step in range(1, GRPS):
            total = total + zbuf[step, at].astype(F32) * msc[step, 0, t].astype(F32)
        acc[t] = total
    acc[tiles] = jnp.zeros((ROWS, T), F32)

    def owned_copy(step):
        target = (me + step) % BLKS
        return pltpu.make_async_remote_copy(
            src_ref=obuf.at[target],
            dst_ref=out.at[0, me],
            send_sem=osend.at[step],
            recv_sem=orecv.at[step],
            device_id=(target, grp),
            device_id_type=MESH,
        )

    def owned_arrival(step):
        source = (me + BLKS - step) % BLKS
        return pltpu.make_async_remote_copy(
            src_ref=obuf.at[source],
            dst_ref=out.at[0, source],
            send_sem=osend.at[step],
            recv_sem=orecv.at[step],
            device_id=(source, grp),
            device_id_type=MESH,
        )

    for step in range(BLKS):
        o = (me + step) % BLKS
        for c in range(SLOTS):
            obuf[o, c] = acc[tbl[o * 2 + c]]
        if step > 0:
            owned_copy(step).start()
    keep = pltpu.make_async_copy(obuf.at[me], out.at[0, me], osem)
    keep.start()

    for part in range(PARTS):
        for k in NEAR:
            raw_copy(part, k).wait_send()
        fitted_copy(part, core).wait_send()
    for q in range(QS):
        for k in NEAR:
            partial_copy(q, k).wait_send()
    for u in range(HALF):
        if ORDER[u] < HALF:
            cross_copy(u).wait_send()
    for step in range(1, GRPS):
        mask_copy(step).wait_send()
        for n, first, last in slices:
            slice_copy(n, first, last, step).wait_send()
    keep.wait()
    for step in range(1, BLKS):
        owned_arrival(step).wait_recv()
        owned_copy(step).wait_send()


def per_device(raw_panels, metric, tile_pairs, owners, group_mask):
    tiles = tile_pairs.shape[0]
    dma = pltpu.SemaphoreType.DMA
    any_space = pl.BlockSpec(memory_space=pl.ANY)
    hbm = pl.BlockSpec(memory_space=pltpu.HBM)
    smem = pl.BlockSpec(memory_space=pltpu.SMEM)
    return pl.pallas_call(
        kernel,
        out_shape=jax.ShapeDtypeStruct((1, BLKS, SLOTS, ROWS, T), F32),
        in_specs=[hbm, hbm, smem, smem, hbm],
        out_specs=any_space,
        scratch_shapes=[
            pltpu.VMEM((K, K), BF16),
            pltpu.VMEM((CHIPS, T, K), BF16),
            pltpu.VMEM((CHIPS, 2, T, K), BF16),
            pltpu.VMEM((CHIPS, HALF, T, T), BF16),
            pltpu.VMEM((CHIPS, HALF, T, T), BF16),
            pltpu.VMEM((HALF, T, T), BF16),
            pltpu.VMEM((BLKS, T, T), BF16),
            pltpu.VMEM((GRPS, BLKS, ROWS, T), BF16),
            pltpu.VMEM((tiles + 1, ROWS, T), F32),
            pltpu.VMEM((BLKS, SLOTS, ROWS, T), F32),
            pltpu.VMEM((GRPS, 1, tiles), jnp.int32),
            pltpu.SMEM((GRPS, 1, tiles), jnp.int32),
            pltpu.SMEM((BLKS * SLOTS,), jnp.int32),
            pltpu.SMEM((BLKS,), jnp.int32),
            dma(()), dma(()), dma(()),
            dma((PARTS, CHIPS)), dma((PARTS, CHIPS)),
            dma((PARTS,)), dma((PARTS,)),
            dma((QS, CHIPS)), dma((QS, CHIPS)),
            dma((HALF,)), dma((HALF,)),
            dma((2 * QS - 1, GRPS)), dma((2 * QS - 1, GRPS)),
            dma((BLKS,)), dma((BLKS,)),
            dma((GRPS,)), dma((GRPS,)),
            dma(()),
        ],
        compiler_params=pltpu.CompilerParams(collective_id=0, has_side_effects=True, vmem_limit_bytes=LIMIT << 20),
        name="exchange",
    )(raw_panels[0], metric, tile_pairs.T, owners.T, group_mask.T)


def solution(mesh):
    placed = (P("grp", "blk", None), P(), P("blk", None), P("blk", None), P("blk", "grp"))
    return jax.shard_map(
        per_device,
        mesh=mesh,
        in_specs=placed,
        out_specs=P("blk", None, None, "grp", None),
        check_vma=False,
    )
```

time: 99.3 us -> 82.1 us (0.83)
  Pallas kernels: 97.5 us -> 80.2 us
    pallas_call x1, Pallas kernels: 97.5 us -> 80.2 us  [per_device(): pl.pallas_call(kernel, out_shape=jax.ShapeDtypeStruct((1, BLKS, SLOTS, RO...]
where the time goes in v2:
time: 82.1 us; the launch traced here: 81.9 us
  Pallas kernels  80.2 us (98%)
  local copies, waits for them, and re-layouts  1.67 us (2%)
    pallas_call x1, Pallas kernels, per_device(): pl.pallas_call(kernel, out_shape=jax.ShapeDtypeStruct((1, BLKS, SLOTS, RO...  80.2 us
    unnamed x1, local copies, waits for them, and re-layouts  1.67 us

profile of v2, /device:TPU:1, one launch (start us, length us, event | category | flops | bytes accessed | tf_op | source)
XLA Modules:
  0.0 81.9 jit_solution(13844596457640102466)
XLA Ops:
  0.0 80.2 %exchange.1 = f32[1,16,2,16,128]{4,3,2,1,0:T(8,128)} custom-call(bf16[128,8192]{1,0:T(8,128)(2,1)} %bitcast.4, bf16[1024,1024]{1,0:T(8,128)(2,1)} %metric.1, s32[2,14]{1,0:T(2,128)} %bitcast.5, s32[1,14]{1,0:T(1,128)} %bitcast.6, s32[1,14]{1,0:T(1,128)} %bitcast.7), custom_call_target="tpu_custom_call" | custom-call | tf_op jit(solution)/shard_map/exchange/pallas_call | solution.py:298
  80.2 1.7 %copy.7 = f32[1,16,2,16,128]{4,3,2,1,0:T(8,128)} copy(f32[1,16,2,16,128]{4,3,2,1,0:T(8,128)} %exchange.1) | data formatting | bytes 524288

commit v3 on v2

--- a/solution.py
+++ b/solution.py
@@ -22,6 +22,7 @@
 ORDER = (2, 4, 6, 1, 3, 5, 7, 8)
 STARTS = (0, 2, 4, 7, 8)
 QS = len(STARTS) - 1
+AHEAD = 3
 LIMIT = 60
 
 
@@ -144,7 +145,7 @@
             device_id_type=MESH,
         )
 
-    def products(q):
+    def products(q, send):
         def multiply(step, carry):
             k = (step + 1) % CHIPS
             target = chip_to(k)
@@ -154,21 +155,28 @@
                 block = (reducer + ORDER[u]) % BLKS
                 sbuf[k, u] = dot_t(fbuf[block // 2, block % 2], right).astype(BF16)
 
-            @pl.when(k > 0)
-            def _():
-                partial_copy(q, k).start()
+            if send:
+
+                @pl.when(k > 0)
+                def _():
+                    partial_copy(q, k).start()
 
             return carry
 
         lax.fori_loop(0, CHIPS, multiply, 0)
 
-    def cross_copy(u):
-        return pltpu.make_async_remote_copy(
-            src_ref=xs.at[u],
-            dst_ref=xall.at[HALF + u],
-            send_sem=xsend.at[u],
-            recv_sem=xrecv.at[u],
-            device_id=((me + ORDER[u]) % BLKS, grp),
+    def ship(q):
+        for k in NEAR:
+            partial_copy(q, k).start()
+
+    def cross_copy(u, step):
+        target = (grp + step) % GRPS
+        return pltpu.make_async_remote_copy(
+            src_ref=xs.at[u, pl.ds(pl.multiple_of(target * ROWS, ROWS), ROWS)],
+            dst_ref=zbuf.at[step, HALF + u],
+            send_sem=xsend.at[u, step],
+            recv_sem=xrecv.at[u, step],
+            device_id=((me + ORDER[u]) % BLKS, target),
             device_id_type=MESH,
         )
 
@@ -191,6 +199,8 @@
         slices.append((n, first, last))
         for step in range(1, GRPS):
             slice_copy(n, first, last, step).start()
+
+    own_rows = pl.ds(pl.multiple_of(grp * ROWS, ROWS), ROWS)
 
     def reduce(q):
         for k in NEAR:
@@ -201,42 +211,50 @@
                 total = total + pbuf[k, u].astype(F32)
             if ORDER[u] < HALF:
                 xs[u] = total.astype(BF16)
-                cross_copy(u).start()
+                for step in range(GRPS):
+                    cross_copy(u, step).start()
             xall[u] = total.T.astype(BF16)
-        send_slices(STARTS[q], STARTS[q + 1])
-
-    def crossed(q):
-        for u in range(STARTS[q], STARTS[q + 1]):
-            cross_copy(u).wait_recv()
-        send_slices(HALF + STARTS[q], HALF + STARTS[q + 1])
-
-    products(0)
+            zbuf[0, u] = xall[u, own_rows, :]
+
+    products(0, True)
     for part in range(PARTS):
         fitted_copy(part, 1 - core).wait_recv()
     for q in range(1, QS):
-        products(q)
-    for q in range(QS):
-        reduce(q)
-        if q > 0:
-            crossed(q - 1)
-
+        products(q, q < AHEAD)
+    for part in range(PARTS):
+        for k in NEAR:
+            raw_copy(part, k).wait_send()
+        fitted_copy(part, core).wait_send()
     for step in range(1, GRPS):
+        mask_copy(step).wait_send()
         mask_copy(step).wait_recv()
     own_mask.wait()
     masks = pltpu.make_async_copy(mvec, msc, vsem)
     masks.start()
     masks.wait()
+    acc[tiles] = jnp.zeros((ROWS, T), F32)
+    for q in range(QS):
+        reduce(q)
+        send_slices(STARTS[q], STARTS[q + 1])
+        if q + AHEAD < QS:
+            ship(q + AHEAD)
+
+    for q in range(QS):
+        for k in NEAR:
+            partial_copy(q, k).wait_send()
     for n, first, last in slices:
         for step in range(1, GRPS):
             slice_copy(n, first, last, step).wait_recv()
-    own_rows = pl.ds(pl.multiple_of(grp * ROWS, ROWS), ROWS)
+    for u in range(HALF):
+        if ORDER[u] < HALF:
+            for step in range(GRPS):
+                cross_copy(u, step).wait_recv()
     for t in range(tiles):
         at = place[(pairs[1, t] - me + BLKS) % BLKS]
-        total = xall[at, own_rows, :].astype(F32) * msc[0, 0, t].astype(F32)
+        total = zbuf[0, at].astype(F32) * msc[0, 0, t].astype(F32)
         for step in range(1, GRPS):
             total = total + zbuf[step, at].astype(F32) * msc[step, 0, t].astype(F32)
         acc[t] = total
-    acc[tiles] = jnp.zeros((ROWS, T), F32)
 
     def owned_copy(step):
         target = (me + step) % BLKS
@@ -269,18 +287,11 @@
     keep = pltpu.make_async_copy(obuf.at[me], out.at[0, me], osem)
     keep.start()
 
-    for part in range(PARTS):
-        for k in NEAR:
-            raw_copy(part, k).wait_send()
-        fitted_copy(part, core).wait_send()
-    for q in range(QS):
-        for k in NEAR:
-            partial_copy(q, k).wait_send()
     for u in range(HALF):
         if ORDER[u] < HALF:
-            cross_copy(u).wait_send()
+            for step in range(GRPS):
+                cross_copy(u, step).wait_send()
     for step in range(1, GRPS):
-        mask_copy(step).wait_send()
         for n, first, last in slices:
             slice_copy(n, first, last, step).wait_send()
     keep.wait()
@@ -307,7 +318,7 @@
             pltpu.VMEM((CHIPS, HALF, T, T), BF16),
             pltpu.VMEM((CHIPS, HALF, T, T), BF16),
             pltpu.VMEM((HALF, T, T), BF16),
-            pltpu.VMEM((BLKS, T, T), BF16),
+            pltpu.VMEM((HALF, T, T), BF16),
             pltpu.VMEM((GRPS, BLKS, ROWS, T), BF16),
             pltpu.VMEM((tiles + 1, ROWS, T), F32),
             pltpu.VMEM((BLKS, SLOTS, ROWS, T), F32),
@@ -319,8 +330,8 @@
             dma((PARTS, CHIPS)), dma((PARTS, CHIPS)),
             dma((PARTS,)), dma((PARTS,)),
             dma((QS, CHIPS)), dma((QS, CHIPS)),
-            dma((HALF,)), dma((HALF,)),
-            dma((2 * QS - 1, GRPS)), dma((2 * QS - 1, GRPS)),
+            dma((HALF, GRPS)), dma((HALF, GRPS)),
+            dma((QS, GRPS)), dma((QS, GRPS)),
             dma((BLKS,)), dma((BLKS,)),
             dma((GRPS,)), dma((GRPS,)),
             dma(()),

time: 82.1 us -> 79.4 us (0.967)
  Pallas kernels: 80.2 us -> 77.6 us
    pallas_call x1, Pallas kernels: 80.2 us -> 77.6 us  [per_device(): pl.pallas_call(kernel, out_shape=jax.ShapeDtypeStruct((1, BLKS, SLOTS, RO...]
where the time goes in v3:
time: 79.4 us; the launch traced here: 79.3 us
  Pallas kernels  77.6 us (98%)
  local copies, waits for them, and re-layouts  1.67 us (2%)
    pallas_call x1, Pallas kernels, per_device(): pl.pallas_call(kernel, out_shape=jax.ShapeDtypeStruct((1, BLKS, SLOTS, RO...  77.6 us
    unnamed x1, local copies, waits for them, and re-layouts  1.67 us

profile of v3, /device:TPU:1, one launch (start us, length us, event | category | flops | bytes accessed | tf_op | source)
XLA Modules:
  0.0 79.3 jit_solution(2266340112138169251)
XLA Ops:
  0.0 77.6 %exchange.1 = f32[1,16,2,16,128]{4,3,2,1,0:T(8,128)} custom-call(bf16[128,8192]{1,0:T(8,128)(2,1)} %bitcast.4, bf16[1024,1024]{1,0:T(8,128)(2,1)} %metric.1, s32[2,14]{1,0:T(2,128)} %bitcast.5, s32[1,14]{1,0:T(1,128)} %bitcast.6, s32[1,14]{1,0:T(1,128)} %bitcast.7), custom_call_target="tpu_custom_call" | custom-call | tf_op jit(solution)/shard_map/exchange/pallas_call | solution.py:309
  77.6 1.7 %copy.7 = f32[1,16,2,16,128]{4,3,2,1,0:T(8,128)} copy(f32[1,16,2,16,128]{4,3,2,1,0:T(8,128)} %exchange.1) | data formatting | bytes 524288

commit v4 on v3

--- a/solution.py
+++ b/solution.py
@@ -20,9 +20,9 @@
 PART = T // PARTS
 NEAR = (2, 6, 1, 5, 3, 7, 4)
 ORDER = (2, 4, 6, 1, 3, 5, 7, 8)
-STARTS = (0, 2, 4, 7, 8)
+STARTS = (0, 3, 6, 7, 8)
 QS = len(STARTS) - 1
-AHEAD = 3
+REACHED = (CHIPS, CHIPS, CHIPS, CHIPS // 2)
 LIMIT = 60
 
 
@@ -47,18 +47,17 @@
     def chip_from(k):
         return ((cx + 4 - k // 2) % 4) * 2 + (cy + k % 2) % 2
 
+    barrier = pltpu.get_barrier_semaphore()
+    for step in range(1, BLKS):
+        pl.semaphore_signal(barrier, inc=1, device_id=((me + step) % BLKS, grp), device_id_type=MESH)
+    for step in range(1, GRPS):
+        pl.semaphore_signal(barrier, inc=1, device_id=(me, (grp + step) % GRPS), device_id_type=MESH)
     fetch_metric = pltpu.make_async_copy(metric, met, msem)
     fetch_metric.start()
     own = pltpu.make_async_copy(raw.at[:, pl.ds(pl.multiple_of(chip * K, K), K)], rbuf.at[0], lsem)
     own.start()
     own_mask = pltpu.make_async_copy(mask, mvec.at[0], vsem)
     own_mask.start()
-
-    barrier = pltpu.get_barrier_semaphore()
-    for step in range(1, BLKS):
-        pl.semaphore_signal(barrier, inc=1, device_id=((me + step) % BLKS, grp), device_id_type=MESH)
-    for step in range(1, GRPS):
-        pl.semaphore_signal(barrier, inc=1, device_id=(me, (grp + step) % GRPS), device_id_type=MESH)
     pl.semaphore_wait(barrier, BLKS - 1 + GRPS - 1)
 
     def raw_copy(part, k):
@@ -134,40 +133,37 @@
 
     lax.fori_loop(0, PARTS, fit, 0)
 
-    def partial_copy(q, k):
+    def reach(q, n):
+        return n if q < QS - 1 else n + n // 2 * 4 * core
+
+    def partial_copy(q, n):
         which = pl.ds(STARTS[q], STARTS[q + 1] - STARTS[q])
         return pltpu.make_async_remote_copy(
-            src_ref=sbuf.at[k, which],
-            dst_ref=pbuf.at[k, which],
-            send_sem=psend.at[q, k],
-            recv_sem=precv.at[q, k],
-            device_id=(chip_to(k) * 2 + core, grp),
-            device_id_type=MESH,
-        )
-
-    def products(q, send):
+            src_ref=sbuf.at[n, which],
+            dst_ref=pbuf.at[n, which],
+            send_sem=psend.at[q, n],
+            recv_sem=precv.at[q, n],
+            device_id=(chip_to(reach(q, n)) * 2 + core, grp),
+            device_id_type=MESH,
+        )
+
+    def products(q):
         def multiply(step, carry):
-            k = (step + 1) % CHIPS
-            target = chip_to(k)
+            n = (step + 1) % REACHED[q]
+            target = chip_to(reach(q, n))
             reducer = target * 2 + core
             right = fbuf[target, core]
             for u in range(STARTS[q], STARTS[q + 1]):
                 block = (reducer + ORDER[u]) % BLKS
-                sbuf[k, u] = dot_t(fbuf[block // 2, block % 2], right).astype(BF16)
-
-            if send:
-
-                @pl.when(k > 0)
-                def _():
-                    partial_copy(q, k).start()
+                sbuf[n, u] = dot_t(fbuf[block // 2, block % 2], right).astype(BF16)
+
+            @pl.when(n > 0)
+            def _():
+                partial_copy(q, n).start()
 
             return carry
 
-        lax.fori_loop(0, CHIPS, multiply, 0)
-
-    def ship(q):
-        for k in NEAR:
-            partial_copy(q, k).start()
+        lax.fori_loop(0, REACHED[q], multiply, 0)
 
     def cross_copy(u, step):
         target = (grp + step) % GRPS
@@ -203,24 +199,23 @@
     own_rows = pl.ds(pl.multiple_of(grp * ROWS, ROWS), ROWS)
 
     def reduce(q):
-        for k in NEAR:
-            partial_copy(q, k).wait_recv()
+        for n in range(1, REACHED[q]):
+            partial_copy(q, n).wait_recv()
         for u in range(STARTS[q], STARTS[q + 1]):
             total = sbuf[0, u].astype(F32)
-            for k in range(1, CHIPS):
-                total = total + pbuf[k, u].astype(F32)
-            if ORDER[u] < HALF:
-                xs[u] = total.astype(BF16)
-                for step in range(GRPS):
-                    cross_copy(u, step).start()
+            for n in range(1, REACHED[q]):
+                total = total + pbuf[n, u].astype(F32)
+            xs[u] = total.astype(BF16)
+            for step in range(GRPS):
+                cross_copy(u, step).start()
             xall[u] = total.T.astype(BF16)
             zbuf[0, u] = xall[u, own_rows, :]
 
-    products(0, True)
+    products(0)
     for part in range(PARTS):
         fitted_copy(part, 1 - core).wait_recv()
     for q in range(1, QS):
-        products(q, q < AHEAD)
+        products(q)
     for part in range(PARTS):
         for k in NEAR:
             raw_copy(part, k).wait_send()
@@ -235,25 +230,28 @@
     acc[tiles] = jnp.zeros((ROWS, T), F32)
     for q in range(QS):
         reduce(q)
-        send_slices(STARTS[q], STARTS[q + 1])
-        if q + AHEAD < QS:
-            ship(q + AHEAD)
+        if q == QS - 3:
+            send_slices(0, STARTS[q + 1])
+        if q == QS - 1:
+            send_slices(STARTS[q - 1], HALF)
 
     for q in range(QS):
-        for k in NEAR:
-            partial_copy(q, k).wait_send()
+        for n in range(1, REACHED[q]):
+            partial_copy(q, n).wait_send()
     for n, first, last in slices:
         for step in range(1, GRPS):
             slice_copy(n, first, last, step).wait_recv()
     for u in range(HALF):
-        if ORDER[u] < HALF:
-            for step in range(GRPS):
-                cross_copy(u, step).wait_recv()
+        for step in range(GRPS):
+            cross_copy(u, step).wait_recv()
     for t in range(tiles):
-        at = place[(pairs[1, t] - me + BLKS) % BLKS]
-        total = zbuf[0, at].astype(F32) * msc[0, 0, t].astype(F32)
-        for step in range(1, GRPS):
-            total = total + zbuf[step, at].astype(F32) * msc[step, 0, t].astype(F32)
+        apart = (pairs[1, t] - me + BLKS) % BLKS
+        at = place[apart]
+        both = (apart == HALF).astype(F32)
+        total = jnp.zeros((ROWS, T), F32)
+        for step in range(GRPS):
+            value = zbuf[step, at].astype(F32) + zbuf[step, BLKS - 1].astype(F32) * both
+            total = total + value * msc[step, 0, t].astype(F32)
         acc[t] = total
 
     def owned_copy(step):
@@ -288,9 +286,8 @@
     keep.start()
 
     for u in range(HALF):
-        if ORDER[u] < HALF:
-            for step in range(GRPS):
-                cross_copy(u, step).wait_send()
+        for step in range(GRPS):
+            cross_copy(u, step).wait_send()
     for step in range(1, GRPS):
         for n, first, last in slices:
             slice_copy(n, first, last, step).wait_send()

time: 79.4 us -> 78.2 us (0.985)
  Pallas kernels: 77.6 us -> 76.3 us
    pallas_call x1, Pallas kernels: 77.6 us -> 76.3 us  [per_device(): pl.pallas_call(kernel, out_shape=jax.ShapeDtypeStruct((1, BLKS, SLOTS, RO...]
where the time goes in v4:
time: 78.2 us; the launch traced here: 78 us
  Pallas kernels  76.3 us (98%)
  local copies, waits for them, and re-layouts  1.67 us (2%)
    pallas_call x1, Pallas kernels, per_device(): pl.pallas_call(kernel, out_shape=jax.ShapeDtypeStruct((1, BLKS, SLOTS, RO...  76.3 us
    unnamed x1, local copies, waits for them, and re-layouts  1.67 us

profile of v4, /device:TPU:1, one launch (start us, length us, event | category | flops | bytes accessed | tf_op | source)
XLA Modules:
  0.0 78.0 jit_solution(16815538153877365122)
XLA Ops:
  0.0 76.3 %exchange.1 = f32[1,16,2,16,128]{4,3,2,1,0:T(8,128)} custom-call(bf16[128,8192]{1,0:T(8,128)(2,1)} %bitcast.4, bf16[1024,1024]{1,0:T(8,128)(2,1)} %metric.1, s32[2,14]{1,0:T(2,128)} %bitcast.5, s32[1,14]{1,0:T(1,128)} %bitcast.6, s32[1,14]{1,0:T(1,128)} %bitcast.7), custom_call_target="tpu_custom_call" | custom-call | tf_op jit(solution)/shard_map/exchange/pallas_call | solution.py:306
  76.3 1.7 %copy.7 = f32[1,16,2,16,128]{4,3,2,1,0:T(8,128)} copy(f32[1,16,2,16,128]{4,3,2,1,0:T(8,128)} %exchange.1) | data formatting | bytes 524288

commit v5 on v4

--- a/solution.py
+++ b/solution.py
@@ -206,10 +206,9 @@
             for n in range(1, REACHED[q]):
                 total = total + pbuf[n, u].astype(F32)
             xs[u] = total.astype(BF16)
-            for step in range(GRPS):
+            for step in (4, 5, 3, 2, 6, 7, 1, 0):
                 cross_copy(u, step).start()
             xall[u] = total.T.astype(BF16)
-            zbuf[0, u] = xall[u, own_rows, :]
 
     products(0)
     for part in range(PARTS):
@@ -234,6 +233,8 @@
             send_slices(0, STARTS[q + 1])
         if q == QS - 1:
             send_slices(STARTS[q - 1], HALF)
+            for u in range(HALF):
+                zbuf[0, u] = xall[u, own_rows, :]
 
     for q in range(QS):
         for n in range(1, REACHED[q]):
@@ -276,7 +277,7 @@
             device_id_type=MESH,
         )
 
-    for step in range(BLKS):
+    for step in (8, 10, 6, 9, 7, 11, 5, 12, 4, 3, 13, 2, 14, 15, 1, 0):
         o = (me + step) % BLKS
         for c in range(SLOTS):
             obuf[o, c] = acc[tbl[o * 2 + c]]

time: 78.2 us -> 78.1 us (level)
  no operation moved by 1% of the time
where the time goes in v5:
time: 78.1 us; the launch traced here: 77.9 us
  Pallas kernels  76.3 us (98%)
  local copies, waits for them, and re-layouts  1.67 us (2%)
    pallas_call x1, Pallas kernels, per_device(): pl.pallas_call(kernel, out_shape=jax.ShapeDtypeStruct((1, BLKS, SLOTS, RO...  76.3 us
    unnamed x1, local copies, waits for them, and re-layouts  1.67 us

profile of v5, /device:TPU:1, one launch (start us, length us, event | category | flops | bytes accessed | tf_op | source)
XLA Modules:
  0.0 77.9 jit_solution(4462275882394854047)
XLA Ops:
  0.0 76.3 %exchange.1 = f32[1,16,2,16,128]{4,3,2,1,0:T(8,128)} custom-call(bf16[128,8192]{1,0:T(8,128)(2,1)} %bitcast.4, bf16[1024,1024]{1,0:T(8,128)(2,1)} %metric.1, s32[2,14]{1,0:T(2,128)} %bitcast.5, s32[1,14]{1,0:T(1,128)} %bitcast.6, s32[1,14]{1,0:T(1,128)} %bitcast.7), custom_call_target="tpu_custom_call" | custom-call | tf_op jit(solution)/shard_map/exchange/pallas_call | solution.py:307
  76.3 1.7 %copy.7 = f32[1,16,2,16,128]{4,3,2,1,0:T(8,128)} copy(f32[1,16,2,16,128]{4,3,2,1,0:T(8,128)} %exchange.1) | data formatting | bytes 524288

commit v6 on v5

--- a/solution.py
+++ b/solution.py
@@ -20,7 +20,7 @@
 PART = T // PARTS
 NEAR = (2, 6, 1, 5, 3, 7, 4)
 ORDER = (2, 4, 6, 1, 3, 5, 7, 8)
-STARTS = (0, 3, 6, 7, 8)
+STARTS = (0, 2, 6, 7, 8)
 QS = len(STARTS) - 1
 REACHED = (CHIPS, CHIPS, CHIPS, CHIPS // 2)
 LIMIT = 60

time: 78.1 us -> 78 us (level)
  no operation moved by 1% of the time
where the time goes in v6:
time: 78 us; the launch traced here: 77.9 us
  Pallas kernels  76.2 us (98%)
  local copies, waits for them, and re-layouts  1.67 us (2%)
    pallas_call x1, Pallas kernels, per_device(): pl.pallas_call(kernel, out_shape=jax.ShapeDtypeStruct((1, BLKS, SLOTS, RO...  76.2 us
    unnamed x1, local copies, waits for them, and re-layouts  1.67 us

profile of v6, /device:TPU:1, one launch (start us, length us, event | category | flops | bytes accessed | tf_op | source)
XLA Modules:
  0.0 77.9 jit_solution(15352074793983853753)
XLA Ops:
  0.0 76.2 %exchange.1 = f32[1,16,2,16,128]{4,3,2,1,0:T(8,128)} custom-call(bf16[128,8192]{1,0:T(8,128)(2,1)} %bitcast.4, bf16[1024,1024]{1,0:T(8,128)(2,1)} %metric.1, s32[2,14]{1,0:T(2,128)} %bitcast.5, s32[1,14]{1,0:T(1,128)} %bitcast.6, s32[1,14]{1,0:T(1,128)} %bitcast.7), custom_call_target="tpu_custom_call" | custom-call | tf_op jit(solution)/shard_map/exchange/pallas_call | solution.py:307
  76.2 1.7 %copy.7 = f32[1,16,2,16,128]{4,3,2,1,0:T(8,128)} copy(f32[1,16,2,16,128]{4,3,2,1,0:T(8,128)} %exchange.1) | data formatting | bytes 524288
